TPU v7x, 32 devices: a whole 2x2x4 slice. The times are simulated.
32 devices in a mesh: row: 16 (over z, y, core), col: 2 (over x).
Axes of the slice: x: 2, y: 2, z: 4, core: 2. Of those that a mesh axis runs over, the one named last changes fastest.
Arguments:
- views: bfloat16 [81, 1024, 512], P(None, 'row', 'col'), may hold values from -6 to 6
Outputs:
- increment: float32 [1024, 512], P('row', 'col')
- residual: float32 [1024, 512], P('row', 'col')
All inputs are finite; a program needn't handle non-finite values.
Results may differ from a plain program's by a relative error of at most 0.0005.
Values may be sent and summed in bfloat16 or wider, within the bound.
A program may use at most 64 MiB of HBM per device.

v0:
```python
import jax
import jax.numpy as jnp
from jax import lax
from jax.sharding import PartitionSpec as P

ANG = 9
VIEWS = 81
D0 = 3
HALO = 13
ITERS = 2


smooth_weight = 2.0
damping = 0.1


def with_halo(array, sides, width):
    for axis, dim in sides:
        count, length = (lax.axis_size(axis), array.shape[dim])
        up = [(i, (i + 1) % count) for i in range(count - 1)]
        down = [(j, i) for i, j in up]
        last = lax.slice_in_dim(array, length - width, length, axis=dim)
        leading = lax.slice_in_dim(array, 0, width, axis=dim)
        before = lax.ppermute(last, axis, up)
        after = lax.ppermute(leading, axis, down)
        array = jnp.concatenate([before, array, after], axis=dim)
    return array


def operate(field, coeff, horiz, verti):
    padded = with_halo(field, (("row", 0), ("col", 1)), 1)
    edges = horiz[:, 1:] * (field - padded[1:-1, 2:]) + horiz[:, :-1] * (field - padded[1:-1, :-2])
    edges = (
        edges + verti[1:] * (field - padded[2:, 1:-1]) + verti[:-1] * (field - padded[:-2, 1:-1])
    )
    return coeff * field + smooth_weight * edges


def shards(views):
    rows_dev = views.shape[1]
    cols_dev = views.shape[2]
    total_rows = rows_dev * lax.axis_size("row")
    total_cols = cols_dev * lax.axis_size("col")
    bands = []
    extended = with_halo(views, (("row", 1), ("col", 2)), HALO)
    for srow_index in range(ANG):
        srow = srow_index - ANG // 2
        start = HALO + D0 * srow - 1
        bands.append(
            extended[srow_index * ANG : (srow_index + 1) * ANG, start : start + rows_dev + 2, :]
        )
    center_ext = bands[ANG // 2][ANG // 2, :, HALO - 1 : HALO + cols_dev + 1].astype(jnp.float32)
    center = center_ext[1:-1, 1:-1]
    data_sum = jnp.zeros((rows_dev, cols_dev), jnp.float32)
    source_sum = jnp.zeros((rows_dev, cols_dev), jnp.float32)
    for srow_index in range(ANG):
        srow = float(srow_index - ANG // 2)
        band = bands[srow_index]
        for tindex in range(ANG):
            tcol = tindex - ANG // 2
            left = HALO + D0 * tcol
            image = band[tindex].astype(jnp.float32)
            warped = image[1:-1, left : left + cols_dev]
            down_diff = 0.5 * (
                image[2:, left : left + cols_dev] - image[:-2, left : left + cols_dev]
            )
            side_diff = 0.5 * (
                image[1:-1, left + 1 : left + 1 + cols_dev]
                - image[1:-1, left - 1 : left - 1 + cols_dev]
            )
            slope = srow * down_diff + tcol * side_diff
            error = warped - center
            robust = 1.0 / jnp.sqrt(1.0 + error * error)
            data_sum = data_sum + robust * slope * slope
            source_sum = source_sum - robust * slope * error
    coeff = damping + data_sum / VIEWS
    source = source_sum / VIEWS
    across = center_ext[1:-1, 1:] - center_ext[1:-1, :-1]
    vertical = center_ext[1:, 1:-1] - center_ext[:-1, 1:-1]
    columns = lax.axis_index("col") * cols_dev + jnp.arange(cols_dev + 1)
    row_index = lax.axis_index("row") * rows_dev + jnp.arange(rows_dev + 1)
    horiz = jnp.where(
        ((columns >= 1) & (columns <= total_cols - 1))[None, :], jnp.exp(-across * across), 0.0
    )
    verti = jnp.where(
        ((row_index >= 1) & (row_index <= total_rows - 1))[:, None],
        jnp.exp(-vertical * vertical),
        0.0,
    )
    precond = coeff + smooth_weight * (horiz[:, 1:] + horiz[:, :-1] + verti[1:] + verti[:-1])
    solution = jnp.zeros_like(source)
    residual = source
    scaled_res = residual / precond
    image_res = operate(scaled_res, coeff, horiz, verti)
    inner_old = None
    step_old = None
    for step in range(ITERS):
        inner_rz, inner_wu = lax.psum(
            (jnp.sum(residual * scaled_res), jnp.sum(image_res * scaled_res)), ("row", "col")
        )
        scaled_img = image_res / precond
        last_step = step + 1 == ITERS
        if not last_step:
            next_image = operate(scaled_img, coeff, horiz, verti)
        if step == 0:
            step_size = inner_rz / inner_wu
            direction = scaled_res
            dir_image = image_res
            dir_scaled = scaled_img
            dir_second = next_image
        else:
            momentum = inner_rz / inner_old
            step_size = inner_rz / (inner_wu - momentum * inner_rz / step_old)
            direction = scaled_res + momentum * direction
            dir_image = image_res + momentum * dir_image
        solution = solution + step_size * direction
        residual = residual - step_size * dir_image
        if not last_step:
            scaled_res = scaled_res - step_size * dir_scaled
            image_res = image_res - step_size * dir_second
        inner_old = inner_rz
        step_old = step_size
    return (solution, residual)


def solution(mesh):
    return jax.shard_map(
        shards,
        mesh=mesh,
        in_specs=(P(None, "row", "col"),),
        out_specs=(P("row", "col"), P("row", "col")),
        check_vma=False,
    )
```

profile of v0, /device:TPU:0, one launch (start us, length us, event | category | flops | bytes accessed | tf_op | source)
XLA Modules:
  0.0 245.1 jit_solution(5993044036869586744)
XLA Ops:
  0.6 1.6 fusion.420
  2.4 1.6 collective-permute-start.1
  4.0 1.0 copy.99
  5.0 3.9 %collective-permute-start = (bf16[81,13,256]{2,0,1:T(8,128)(2,1)}, bf16[81,13,256]{2,0,1:T(8,128)(2,1)}, u32[]{:S(2)}, u32[]{:S(2)}) collective-permute-start(bf16[81,13,256]{2,0,1:T(8,128)(2,1)} %copy.99), channel_id=1, source_target_pairs={{0,2},{2,4},{4,6},{6,8},{8,10},{10,12},{12,14},{14,16},{16,18},{18... | collective-permute-start | bytes 1617416 | tf_op jit(solution)/shard_map/ppermute | solution.py:24
  8.8 1.2 copy.94
  10.0 1.2 copy.93
  11.2 0.8 copy-done.3
  12.1 2.0 pad_maximum_fusion
  14.1 2.9 %fusion.419 = (bf16[81,90,13]{2,1,0:T(8,128)(2,1)}, bf16[81,90,13]{2,1,0:T(8,128)(2,1)}) fusion(bf16[81,90,256]{2,1,0:T(8,128)(2,1)S(1)} %pad_maximum_fusion), kind=kLoop, calls=%fused_computation.781 | loop fusion | bytes 758160 | tf_op jit(solution)/shard_map/slice | solution.py:22
  17.0 3.0 %copy.95 = bf16[81,90,13]{1,0,2:T(8,128)(2,1)} copy(bf16[81,90,13]{2,1,0:T(8,128)(2,1)} %get-tuple-element.180) | data formatting | bytes 379080 | tf_op jit(solution)/shard_map/slice | solution.py:22
  19.9 3.0 %copy.96 = bf16[81,90,13]{1,0,2:T(8,128)(2,1)} copy(bf16[81,90,13]{2,1,0:T(8,128)(2,1)} %get-tuple-element.181) | data formatting | bytes 379080 | tf_op jit(solution)/shard_map/slice | solution.py:23
  22.9 1.3 collective-permute-start.3
  24.2 6.3 %collective-permute-start.2 = (bf16[81,90,13]{1,0,2:T(8,128)(2,1)}, bf16[81,90,13]{1,0,2:T(8,128)(2,1)}, u32[]{:S(2)}, u32[]{:S(2)}) collective-permute-start(bf16[81,90,13]{1,0,2:T(8,128)(2,1)} %copy.95), channel_id=1, source_target_pairs={{0,1},{2,3},{4,5},{6,7},{8,9},{10,11},{12,13},{14,15},{16,17},{18,... | collective-permute-start | bytes 568628 | tf_op jit(solution)/shard_map/ppermute | solution.py:24
  30.5 3.8 %collective-permute-done.2 = bf16[81,90,13]{1,0,2:T(8,128)(2,1)} collective-permute-done((bf16[81,90,13]{1,0,2:T(8,128)(2,1)}, bf16[81,90,13]{1,0,2:T(8,128)(2,1)}, u32[]{:S(2)}, u32[]{:S(2)}) %collective-permute-start.2) | collective-permute-done | bytes 189572 | tf_op jit(solution)/shard_map/ppermute | solution.py:24
  34.3 2.9 %copy.97 = bf16[81,90,13]{2,1,0:T(8,128)(2,1)} copy(bf16[81,90,13]{1,0,2:T(8,128)(2,1)} %collective-permute-done.2) | data formatting | bytes 379080 | tf_op jit(solution)/shard_map/ppermute | solution.py:24
  37.3 2.9 %copy.98 = bf16[81,90,13]{2,1,0:T(8,128)(2,1)} copy(bf16[81,90,13]{1,0,2:T(8,128)(2,1)} %collective-permute-done.3) | data formatting | bytes 379080 | tf_op jit(solution)/shard_map/ppermute | solution.py:25
  40.2 1.0 fusion.330
  41.2 0.6 copy-done.1
  41.7 0.6 copy-done.2
  42.5 0.8 fusion.262
  43.3 0.9 fusion.268
  44.2 0.9 fusion.307
  45.1 0.9 fusion.289
  46.0 0.9 fusion.277
  46.8 0.9 fusion.310
  47.7 0.9 fusion.259
  48.6 0.9 fusion.292
  49.5 0.9 fusion.313
  50.3 0.9 fusion.253
  51.2 0.9 fusion.280
  52.1 0.9 fusion.316
  52.9 0.9 fusion.295
  53.8 0.9 fusion.271
  54.7 0.9 fusion.319
  55.5 0.9 fusion.265
  56.4 0.9 fusion.298
  57.3 0.9 fusion.322
  58.2 0.9 fusion.283
  59.0 0.9 fusion.256
  59.9 0.9 fusion.325
  60.8 0.9 fusion.301
  61.7 0.9 fusion.274
  62.5 0.9 fusion.328
  63.4 0.9 fusion.286
  64.3 0.9 fusion.304
  65.1 0.9 fusion.250
  66.5 39.3 %subtract_multiply_fusion = (f32[64,256]{1,0:T(8,128)}, f32[64,256]{1,0:T(8,128)}, f32[64,256]{1,0:T(8,128)}, f32[64,256]{1,0:T(8,128)}, f32[64,256]{1,0:T(8,128...) fusion(f32[66,282]{1,0:T(8,128)} %get-tuple-element.179, ...), kind=kLoop, calls=%fused_computation.525 | loop fusion | flops 14188544 | bytes 31981568 | tf_op jit(solution)/shard_map/div | solution.py:77
  106.1 7.2 %fusion.337 = (f32[64,256]{1,0:T(8,128)S(1)}, f32[64,256]{1,0:T(8,128)S(1)}, f32[64,256]{1,0:T(8,128)S(1)}) fusion(f32[64,256]{1,0:T(8,128)} %get-tuple-element.17, f32[65,256]{1,0:T(8,128)S(1)} %fusion.3, f32[64,257]{1,0:T(8,128)S(1)} %fusion.1, f32[64,256]{1,0:T(8,128)} %get-tuple-element.98, f32[66,282]{1,0:T(8,128)} %get-tuple-element.99, ...), kind=kLoop, calls=%fused_computation.780 | loop fusion | flops 8077312 | bytes 11206656 | tf_op jit(solution)/shard_map/div | solution.py:93
  113.3 1.4 collective-permute-start.5
  114.8 12.8 %collective-permute-start.4 = (f32[1,256]{1,0:T(1,128)S(1)}, f32[1,256]{1,0:T(1,128)S(1)}, u32[]{:S(2)}, u32[]{:S(2)}) collective-permute-start(f32[1,256]{1,0:T(1,128)S(1)} %get-tuple-element.191), channel_id=1, source_target_pairs={{0,2},{2,4},{4,6},{6,8},{8,10},{10,12},{12,14},{14,16},{16,18},{18... | collective-permute-start | bytes 3080 | tf_op jit(solution)/shard_map/ppermute | solution.py:24
  127.6 0.8 collective-permute-done.4
  128.5 1.3 collective-permute-start.6
  129.8 4.5 %collective-permute-start.7 = (f32[66,1]{1,0:T(8,128)S(1)}, f32[66,1]{1,0:T(8,128)S(1)}, u32[]{:S(2)}, u32[]{:S(2)}) collective-permute-start(f32[66,1]{1,0:T(8,128)S(1)} %get-tuple-element.187), channel_id=1, source_target_pairs={{0,1},{2,3},{4,5},{6,7},{8,9},{10,11},{12,13},{14,15},{16,17},{18,... | collective-permute-start | bytes 800 | tf_op jit(solution)/shard_map/ppermute | solution.py:24
  134.3 1.6 collective-permute-done.7
  135.9 0.8 multiply_reduce_fusion.2
  136.8 1.3 collective-permute-start.9
  138.1 5.0 %collective-permute-start.8 = (f32[1,256]{1,0:T(1,128)S(1)}, f32[1,256]{1,0:T(1,128)S(1)}, u32[]{:S(2)}, u32[]{:S(2)}) collective-permute-start(f32[1,256]{1,0:T(1,128)S(1)} %get-tuple-element.189), channel_id=1, source_target_pairs={{0,2},{2,4},{4,6},{6,8},{8,10},{10,12},{12,14},{14,16},{16,18},{18... | collective-permute-start | bytes 3080 | tf_op jit(solution)/shard_map/ppermute | solution.py:24
  143.2 0.8 collective-permute-done.8
  144.0 1.3 collective-permute-start.10
  145.3 4.5 %collective-permute-start.11 = (f32[66,1]{1,0:T(8,128)S(1)}, f32[66,1]{1,0:T(8,128)S(1)}, u32[]{:S(2)}, u32[]{:S(2)}) collective-permute-start(f32[66,1]{1,0:T(8,128)S(1)} %get-tuple-element.185), channel_id=1, source_target_pairs={{0,1},{2,3},{4,5},{6,7},{8,9},{10,11},{12,13},{14,15},{16,17},{18,... | collective-permute-start | bytes 800 | tf_op jit(solution)/shard_map/ppermute | solution.py:24
  149.9 45.2 %all-reduce.1 = (f32[]{:T(128)}, f32[]{:T(128)}) all-reduce(f32[]{:T(128)} %get-tuple-element.7, f32[]{:T(128)} %get-tuple-element.6), channel_id=1, replica_groups=mesh['row'=16,'col'=2] {'row','col'}, use_global_device_ids=true, to_apply=%region_1.2 | all-reduce | flops 2 | bytes 16 | tf_op jit(solution)/shard_map/psum | solution.py:98
  196.4 1.7 multiply_reduce_fusion
  198.1 41.1 %all-reduce = (f32[]{:T(128)}, f32[]{:T(128)}) all-reduce(f32[]{:T(128)} %get-tuple-element.5, f32[]{:T(128)} %get-tuple-element.4), channel_id=1, replica_groups=mesh['row'=16,'col'=2] {'row','col'}, use_global_device_ids=true, to_apply=%region_5.6 | all-reduce | flops 2 | bytes 16 | tf_op jit(solution)/shard_map/psum | solution.py:98
  243.6 1.5 multiply_subtract_fusion
  (91 shorter events, 0.9 us)
Async XLA Ops:
  2.4 9.7 %copy-start = (bf16[81,64,256]{2,1,0:T(8,128)(2,1)S(1)}, bf16[81,64,256]{2,1,0:T(8,128)(2,1)}, u32[]{:S(2)}) copy-start(bf16[81,64,256]{2,1,0:T(8,128)(2,1)} %param.1) | copy-start | bytes 7962628
  2.4 6.4 %collective-permute-start.1 = (bf16[81,13,256]{2,0,1:T(8,128)(2,1)S(1)}, bf16[81,13,256]{2,0,1:T(8,128)(2,1)}, u32[]{:S(2)}, u32[]{:S(2)}) collective-permute-start(bf16[81,13,256]{2,0,1:T(8,128)(2,1)S(1)} %copy.100), channel_id=1, source_target_pairs={{2,0},{4,2},{6,4},{8,6},{10,8},{12,10},{14,12},{16,14},{18,16},{20... | collective-permute-start | bytes 1617416 | tf_op jit(solution)/shard_map/ppermute | solution.py:25
  5.0 5.1 %collective-permute-start = (bf16[81,13,256]{2,0,1:T(8,128)(2,1)}, bf16[81,13,256]{2,0,1:T(8,128)(2,1)}, u32[]{:S(2)}, u32[]{:S(2)}) collective-permute-start(bf16[81,13,256]{2,0,1:T(8,128)(2,1)} %copy.99), channel_id=1, source_target_pairs={{0,2},{2,4},{4,6},{6,8},{8,10},{10,12},{12,14},{14,16},{16,18},{18... | collective-permute-start | bytes 1617416 | tf_op jit(solution)/shard_map/ppermute | solution.py:24
  11.2 0.9 copy-start.3
  22.9 14.3 %collective-permute-start.3 = (bf16[81,90,13]{1,0,2:T(8,128)(2,1)}, bf16[81,90,13]{1,0,2:T(8,128)(2,1)}, u32[]{:S(2)}, u32[]{:S(2)}) collective-permute-start(bf16[81,90,13]{1,0,2:T(8,128)(2,1)} %copy.96), channel_id=1, source_target_pairs={{1,0},{3,2},{5,4},{7,6},{9,8},{11,10},{13,12},{15,14},{17,16},{19,... | collective-permute-start | bytes 568628 | tf_op jit(solution)/shard_map/ppermute | solution.py:25
  24.2 10.1 %collective-permute-start.2 = (bf16[81,90,13]{1,0,2:T(8,128)(2,1)}, bf16[81,90,13]{1,0,2:T(8,128)(2,1)}, u32[]{:S(2)}, u32[]{:S(2)}) collective-permute-start(bf16[81,90,13]{1,0,2:T(8,128)(2,1)} %copy.95), channel_id=1, source_target_pairs={{0,1},{2,3},{4,5},{6,7},{8,9},{10,11},{12,13},{14,15},{16,17},{18,... | collective-permute-start | bytes 568628 | tf_op jit(solution)/shard_map/ppermute | solution.py:24
  40.2 1.6 copy-start.1
  40.2 2.2 copy-start.2
  40.2 2.3 copy-start.4
  66.2 39.6 %copy-start.5 = (f32[66,282]{1,0:T(8,128)S(1)}, f32[66,282]{1,0:T(8,128)}, u32[]{:S(2)}) copy-start(f32[66,282]{1,0:T(8,128)} %get-tuple-element.112) | copy-start | bytes 223348
  66.2 39.6 %copy-start.6 = (f32[66,282]{1,0:T(8,128)S(1)}, f32[66,282]{1,0:T(8,128)}, u32[]{:S(2)}) copy-start(f32[66,282]{1,0:T(8,128)} %get-tuple-element.113) | copy-start | bytes 223348
  66.3 39.6 %copy-start.7 = (f32[66,282]{1,0:T(8,128)S(1)}, f32[66,282]{1,0:T(8,128)}, u32[]{:S(2)}) copy-start(f32[66,282]{1,0:T(8,128)} %get-tuple-element.117) | copy-start | bytes 223348
  66.3 39.6 %copy-start.8 = (f32[66,282]{1,0:T(8,128)S(1)}, f32[66,282]{1,0:T(8,128)}, u32[]{:S(2)}) copy-start(f32[66,282]{1,0:T(8,128)} %get-tuple-element.118) | copy-start | bytes 223348
  66.3 39.6 %copy-start.9 = (f32[66,282]{1,0:T(8,128)S(1)}, f32[66,282]{1,0:T(8,128)}, u32[]{:S(2)}) copy-start(f32[66,282]{1,0:T(8,128)} %get-tuple-element.119) | copy-start | bytes 223348
  66.3 39.6 %copy-start.10 = (f32[66,282]{1,0:T(8,128)S(1)}, f32[66,282]{1,0:T(8,128)}, u32[]{:S(2)}) copy-start(f32[66,282]{1,0:T(8,128)} %get-tuple-element.156) | copy-start | bytes 223348
  66.3 39.6 %copy-start.11 = (f32[66,282]{1,0:T(8,128)S(1)}, f32[66,282]{1,0:T(8,128)}, u32[]{:S(2)}) copy-start(f32[66,282]{1,0:T(8,128)} %get-tuple-element.157) | copy-start | bytes 223348
  66.3 39.6 %copy-start.12 = (f32[66,282]{1,0:T(8,128)S(1)}, f32[66,282]{1,0:T(8,128)}, u32[]{:S(2)}) copy-start(f32[66,282]{1,0:T(8,128)} %get-tuple-element.158) | copy-start | bytes 223348
  66.3 39.6 %copy-start.13 = (f32[66,282]{1,0:T(8,128)S(1)}, f32[66,282]{1,0:T(8,128)}, u32[]{:S(2)}) copy-start(f32[66,282]{1,0:T(8,128)} %get-tuple-element.138) | copy-start | bytes 223348
  66.3 39.6 %copy-start.14 = (f32[66,282]{1,0:T(8,128)S(1)}, f32[66,282]{1,0:T(8,128)}, u32[]{:S(2)}) copy-start(f32[66,282]{1,0:T(8,128)} %get-tuple-element.139) | copy-start | bytes 223348
  66.3 39.6 %copy-start.15 = (f32[66,282]{1,0:T(8,128)S(1)}, f32[66,282]{1,0:T(8,128)}, u32[]{:S(2)}) copy-start(f32[66,282]{1,0:T(8,128)} %get-tuple-element.140) | copy-start | bytes 223348
  66.3 39.6 %copy-start.16 = (f32[66,282]{1,0:T(8,128)S(1)}, f32[66,282]{1,0:T(8,128)}, u32[]{:S(2)}) copy-start(f32[66,282]{1,0:T(8,128)} %get-tuple-element.126) | copy-start | bytes 223348
  66.4 39.6 %copy-start.17 = (f32[66,282]{1,0:T(8,128)S(1)}, f32[66,282]{1,0:T(8,128)}, u32[]{:S(2)}) copy-start(f32[66,282]{1,0:T(8,128)} %get-tuple-element.127) | copy-start | bytes 223348
  66.4 39.6 %copy-start.18 = (f32[66,282]{1,0:T(8,128)S(1)}, f32[66,282]{1,0:T(8,128)}, u32[]{:S(2)}) copy-start(f32[66,282]{1,0:T(8,128)} %get-tuple-element.128) | copy-start | bytes 223348
  66.4 39.6 %copy-start.19 = (f32[66,282]{1,0:T(8,128)S(1)}, f32[66,282]{1,0:T(8,128)}, u32[]{:S(2)}) copy-start(f32[66,282]{1,0:T(8,128)} %get-tuple-element.159) | copy-start | bytes 223348
  66.4 39.6 %copy-start.20 = (f32[66,282]{1,0:T(8,128)S(1)}, f32[66,282]{1,0:T(8,128)}, u32[]{:S(2)}) copy-start(f32[66,282]{1,0:T(8,128)} %get-tuple-element.160) | copy-start | bytes 223348
  66.4 39.6 %copy-start.21 = (f32[66,282]{1,0:T(8,128)S(1)}, f32[66,282]{1,0:T(8,128)}, u32[]{:S(2)}) copy-start(f32[66,282]{1,0:T(8,128)} %get-tuple-element.161) | copy-start | bytes 223348
  66.4 39.6 %copy-start.22 = (f32[66,282]{1,0:T(8,128)S(1)}, f32[66,282]{1,0:T(8,128)}, u32[]{:S(2)}) copy-start(f32[66,282]{1,0:T(8,128)} %get-tuple-element.108) | copy-start | bytes 223348
  66.4 39.6 %copy-start.23 = (f32[66,282]{1,0:T(8,128)S(1)}, f32[66,282]{1,0:T(8,128)}, u32[]{:S(2)}) copy-start(f32[66,282]{1,0:T(8,128)} %get-tuple-element.109) | copy-start | bytes 223348
  66.4 39.6 %copy-start.24 = (f32[66,282]{1,0:T(8,128)S(1)}, f32[66,282]{1,0:T(8,128)}, u32[]{:S(2)}) copy-start(f32[66,282]{1,0:T(8,128)} %get-tuple-element.110) | copy-start | bytes 223348
  66.4 39.6 %copy-start.25 = (f32[66,282]{1,0:T(8,128)S(1)}, f32[66,282]{1,0:T(8,128)}, u32[]{:S(2)}) copy-start(f32[66,282]{1,0:T(8,128)} %get-tuple-element.141) | copy-start | bytes 223348
  66.4 39.6 %copy-start.26 = (f32[66,282]{1,0:T(8,128)S(1)}, f32[66,282]{1,0:T(8,128)}, u32[]{:S(2)}) copy-start(f32[66,282]{1,0:T(8,128)} %get-tuple-element.142) | copy-start | bytes 223348
  66.5 39.6 %copy-start.27 = (f32[66,282]{1,0:T(8,128)S(1)}, f32[66,282]{1,0:T(8,128)}, u32[]{:S(2)}) copy-start(f32[66,282]{1,0:T(8,128)} %get-tuple-element.143) | copy-start | bytes 223348
  66.5 39.6 %copy-start.28 = (f32[66,282]{1,0:T(8,128)S(1)}, f32[66,282]{1,0:T(8,128)}, u32[]{:S(2)}) copy-start(f32[66,282]{1,0:T(8,128)} %get-tuple-element.162) | copy-start | bytes 223348
  66.5 39.6 %copy-start.29 = (f32[66,282]{1,0:T(8,128)S(1)}, f32[66,282]{1,0:T(8,128)}, u32[]{:S(2)}) copy-start(f32[66,282]{1,0:T(8,128)} %get-tuple-element.163) | copy-start | bytes 223348
  66.5 39.6 %copy-start.30 = (f32[66,282]{1,0:T(8,128)S(1)}, f32[66,282]{1,0:T(8,128)}, u32[]{:S(2)}) copy-start(f32[66,282]{1,0:T(8,128)} %get-tuple-element.164) | copy-start | bytes 223348
  66.5 39.6 %copy-start.31 = (f32[66,282]{1,0:T(8,128)S(1)}, f32[66,282]{1,0:T(8,128)}, u32[]{:S(2)}) copy-start(f32[66,282]{1,0:T(8,128)} %get-tuple-element.102) | copy-start | bytes 223348
  66.5 39.6 %copy-start.32 = (f32[66,282]{1,0:T(8,128)S(1)}, f32[66,282]{1,0:T(8,128)}, u32[]{:S(2)}) copy-start(f32[66,282]{1,0:T(8,128)} %get-tuple-element.103) | copy-start | bytes 223348
  106.1 29.9 %copy-start.34 = (f32[64,256]{1,0:T(8,128)S(1)}, f32[64,256]{1,0:T(8,128)}, u32[]{:S(2)}) copy-start(f32[64,256]{1,0:T(8,128)} %get-tuple-element.17) | copy-start | bytes 196612
  113.3 22.6 %copy-start.33 = (f32[64,256]{1,0:T(8,128)}, f32[64,256]{1,0:T(8,128)S(1)}, u32[]{:S(2)}) copy-start(f32[64,256]{1,0:T(8,128)S(1)} %get-tuple-element.14) | copy-start | bytes 196612
  113.3 23.5 %copy-start.36 = (f32[64,256]{1,0:T(8,128)}, f32[64,256]{1,0:T(8,128)S(1)}, u32[]{:S(2)}) copy-start(f32[64,256]{1,0:T(8,128)S(1)} %get-tuple-element.16) | copy-start | bytes 196612
  113.3 130.3 %copy-start.35 = (f32[64,256]{1,0:T(8,128)S(1)}, f32[64,256]{1,0:T(8,128)}, u32[]{:S(2)}) copy-start(f32[64,256]{1,0:T(8,128)} %get-tuple-element.17) | copy-start | bytes 196612
  113.3 14.2 %collective-permute-start.5 = (f32[1,256]{1,0:T(1,128)S(1)}, f32[1,256]{1,0:T(1,128)S(1)}, u32[]{:S(2)}, u32[]{:S(2)}) collective-permute-start(f32[1,256]{1,0:T(1,128)S(1)} %get-tuple-element.190), channel_id=1, source_target_pairs={{2,0},{4,2},{6,4},{8,6},{10,8},{12,10},{14,12},{16,14},{18,16},{20... | collective-permute-start | bytes 3080 | tf_op jit(solution)/shard_map/ppermute | solution.py:25
  114.8 13.6 %collective-permute-start.4 = (f32[1,256]{1,0:T(1,128)S(1)}, f32[1,256]{1,0:T(1,128)S(1)}, u32[]{:S(2)}, u32[]{:S(2)}) collective-permute-start(f32[1,256]{1,0:T(1,128)S(1)} %get-tuple-element.191), channel_id=1, source_target_pairs={{0,2},{2,4},{4,6},{6,8},{8,10},{10,12},{12,14},{14,16},{16,18},{18... | collective-permute-start | bytes 3080 | tf_op jit(solution)/shard_map/ppermute | solution.py:24
  128.5 5.8 %collective-permute-start.6 = (f32[66,1]{1,0:T(8,128)S(1)}, f32[66,1]{1,0:T(8,128)S(1)}, u32[]{:S(2)}, u32[]{:S(2)}) collective-permute-start(f32[66,1]{1,0:T(8,128)S(1)} %get-tuple-element.186), channel_id=1, source_target_pairs={{1,0},{3,2},{5,4},{7,6},{9,8},{11,10},{13,12},{15,14},{17,16},{19,... | collective-permute-start | bytes 800 | tf_op jit(solution)/shard_map/ppermute | solution.py:25
  129.8 6.2 %collective-permute-start.7 = (f32[66,1]{1,0:T(8,128)S(1)}, f32[66,1]{1,0:T(8,128)S(1)}, u32[]{:S(2)}, u32[]{:S(2)}) collective-permute-start(f32[66,1]{1,0:T(8,128)S(1)} %get-tuple-element.187), channel_id=1, source_target_pairs={{0,1},{2,3},{4,5},{6,7},{8,9},{10,11},{12,13},{14,15},{16,17},{18,... | collective-permute-start | bytes 800 | tf_op jit(solution)/shard_map/ppermute | solution.py:24
  136.8 6.4 %collective-permute-start.9 = (f32[1,256]{1,0:T(1,128)S(1)}, f32[1,256]{1,0:T(1,128)S(1)}, u32[]{:S(2)}, u32[]{:S(2)}) collective-permute-start(f32[1,256]{1,0:T(1,128)S(1)} %get-tuple-element.188), channel_id=1, source_target_pairs={{2,0},{4,2},{6,4},{8,6},{10,8},{12,10},{14,12},{16,14},{18,16},{20... | collective-permute-start | bytes 3080 | tf_op jit(solution)/shard_map/ppermute | solution.py:25
  138.1 5.9 %collective-permute-start.8 = (f32[1,256]{1,0:T(1,128)S(1)}, f32[1,256]{1,0:T(1,128)S(1)}, u32[]{:S(2)}, u32[]{:S(2)}) collective-permute-start(f32[1,256]{1,0:T(1,128)S(1)} %get-tuple-element.189), channel_id=1, source_target_pairs={{0,2},{2,4},{4,6},{6,8},{8,10},{10,12},{12,14},{14,16},{16,18},{18... | collective-permute-start | bytes 3080 | tf_op jit(solution)/shard_map/ppermute | solution.py:24
  144.0 52.3 %collective-permute-start.10 = (f32[66,1]{1,0:T(8,128)S(1)}, f32[66,1]{1,0:T(8,128)S(1)}, u32[]{:S(2)}, u32[]{:S(2)}) collective-permute-start(f32[66,1]{1,0:T(8,128)S(1)} %get-tuple-element.184), channel_id=1, source_target_pairs={{1,0},{3,2},{5,4},{7,6},{9,8},{11,10},{13,12},{15,14},{17,16},{19,... | collective-permute-start | bytes 800 | tf_op jit(solution)/shard_map/ppermute | solution.py:25
  145.3 51.0 %collective-permute-start.11 = (f32[66,1]{1,0:T(8,128)S(1)}, f32[66,1]{1,0:T(8,128)S(1)}, u32[]{:S(2)}, u32[]{:S(2)}) collective-permute-start(f32[66,1]{1,0:T(8,128)S(1)} %get-tuple-element.185), channel_id=1, source_target_pairs={{0,1},{2,3},{4,5},{6,7},{8,9},{10,11},{12,13},{14,15},{16,17},{18,... | collective-permute-start | bytes 800 | tf_op jit(solution)/shard_map/ppermute | solution.py:24
where the time goes:
time: 246 us; the launch traced here: 245 us
  blocking collectives  86.3 us (35%)
  other arithmetic  77.3 us (31%)
  starting transfers between devices  45.2 us (18%)
  local copies, waits for them, and re-layouts  22.3 us (9%)
  between operations  7.04 us (3%)
  waiting for transfers between devices  7 us (3%)
    psum x2, blocking collectives, shards(): lax.psum((jnp.sum(residual * scaled_res), jnp.sum(image_res * scaled_res)...  86.3 us
    div x1, other arithmetic, shards(): source = source_sum / VIEWS  39.3 us
    ppermute x6, starting transfers between devices, with_halo(): before = lax.ppermute(last, axis, up)  37.1 us
    convert_element_type x27, other arithmetic, shards(): image = band[tindex].astype(jnp.float32)  23.5 us
    ppermute x6, starting transfers between devices, with_halo(): after = lax.ppermute(leading, axis, down)  8.12 us
    slice x3, local copies, waits for them, and re-layouts, with_halo(): last = lax.slice_in_dim(array, length - width, length, axis=dim)  7.42 us
    div x1, other arithmetic, shards(): scaled_res = residual / precond  7.19 us
    ppermute x6, waiting for transfers between devices, with_halo(): before = lax.ppermute(last, axis, up)  6.99 us
  transfers between devices with their start and end apart: 12, of which 4 were waited for; matrix products, arithmetic and copies ran while one was open for 2% of the time, Pallas kernels for 0%

commit v1 on v0

v1 whole, which is shorter than its diff:
```python
import functools

import jax
import jax.numpy as jnp
from jax import lax
from jax.experimental import pallas as pl
from jax.experimental.pallas import tpu as pltpu
from jax.sharding import PartitionSpec as P

ANG = 9
VIEWS = 81
HALF = 4
CENTER = 40
D0 = 3
smooth_weight = 2.0
damping = 0.1
PAD = 16
LANES = 128
F32 = jnp.float32
DIRS = ((-1, 0), (1, 0), (0, -1), (0, 1), (-1, -1), (-1, 1), (1, -1), (1, 1))


def roll(x, shift):
    return pltpu.roll(x, shift % LANES, 1)


def lane_of(rows):
    return lax.broadcasted_iota(jnp.int32, (rows, LANES), 1)


def kernel(nrow, ncol, views, inc, res, ext, sp, col_r, col_l, fb, pb, cen, cpack, acc, pacc, own, zc, gpack,
           ghost_u, ghost_d, ghost_l, ghost_r, corner, redbuf, redout, load_sem, send1, recv1, send2, recv2, rsend, rrecv):
    rows, cols = views.shape[1], views.shape[2]
    r, c = lax.axis_index("row"), lax.axis_index("col")
    count = nrow * ncol
    me = r * ncol + c
    full = PAD + rows + PAD

    def exists(dr, dc):
        return (r + dr >= 0) & (r + dr < nrow) & (c + dc >= 0) & (c + dc < ncol)

    barrier = pltpu.get_barrier_semaphore()

    def greet(i, carry):
        peer = (me + i) % count
        pl.semaphore_signal(barrier, inc=1, device_id=(peer // ncol, peer % ncol), device_id_type=pl.DeviceIdType.MESH)
        return carry

    lax.fori_loop(1, count, greet, 0)

    loads = []
    for si in range(ANG):
        part = pl.ds(si * ANG, ANG)
        copy = pltpu.make_async_copy(views.at[part], ext.at[part, pl.ds(PAD, rows), :], load_sem.at[si])
        copy.start()
        loads.append(copy)

    def zero(ref, first, number, row, size):
        def body(i, carry):
            ref[first + i, row : row + size, :] = jnp.zeros((size, ref.shape[2]), ref.dtype)
            return carry
        lax.fori_loop(0, number, body, 0)

    @pl.when(r == 0)
    def _():
        zero(ext, 0, 41, 0, PAD)

    @pl.when(r == nrow - 1)
    def _():
        zero(ext, 40, 41, PAD + rows, PAD)

    for ref, edge in ((col_r, c == ncol - 1), (col_l, c == 0)):
        @pl.when(edge)
        def _():
            zero(ref, 0, 10, PAD, rows)

        @pl.when(edge | (r == 0))
        def _():
            zero(ref, 0, 6, 0, PAD)

        @pl.when(edge | (r == nrow - 1))
        def _():
            zero(ref, 5, 5, PAD + rows, PAD)

    for edge, ref in ((r == 0, ghost_u), (r == nrow - 1, ghost_d)):
        @pl.when(edge)
        def _():
            ref[0] = jnp.zeros((8, cols), F32)
            ref[1] = jnp.ones((8, cols), F32)
    for edge, ref, low in ((c == 0, ghost_l, 1.0), (c == ncol - 1, ghost_r, 0.0)):
        @pl.when(edge)
        def _():
            ref[...] = jnp.where(lane_of(rows) < 64, low, 1.0 - low)
    for index, (dr, dc) in enumerate(DIRS[4:]):
        @pl.when(jnp.logical_not(exists(-dr, -dc)))
        def _():
            corner[index] = jnp.zeros((8, LANES), F32)

    pl.semaphore_wait(barrier, count - 1)

    up_rows, down_rows = pl.ds(0, PAD), pl.ds(rows - PAD, PAD)
    copies = []
    for index, (dr, dc) in enumerate(DIRS):
        if dc == 0:
            if dr < 0:
                src, dst = views.at[pl.ds(40, 41), up_rows, :], ext.at[pl.ds(40, 41), pl.ds(PAD + rows, PAD), :]
            else:
                src, dst = views.at[pl.ds(0, 41), down_rows, :], ext.at[pl.ds(0, 41), pl.ds(0, PAD), :]
        else:
            side = col_r if dc < 0 else col_l
            if dr == 0:
                src, dst = sp, side.at[:, pl.ds(PAD, rows), :]
            elif dr < 0:
                src, dst = sp.at[pl.ds(5, 5), up_rows, :], side.at[pl.ds(5, 5), pl.ds(PAD + rows, PAD), :]
            else:
                src, dst = sp.at[pl.ds(0, 6), down_rows, :], side.at[pl.ds(0, 6), pl.ds(0, PAD), :]
        copies.append((dr, dc, pltpu.make_async_remote_copy(
            src_ref=src, dst_ref=dst, send_sem=send1.at[index], recv_sem=recv1.at[index],
            device_id=(r + dr, c + dc), device_id_type=pl.DeviceIdType.MESH)))

    def start(group):
        for dr, dc, copy in group:
            @pl.when(exists(dr, dc))
            def _():
                copy.start()

    def arrive(group):
        for dr, dc, copy in group:
            @pl.when(exists(-dr, -dc))
            def _():
                copy.wait_recv()

    def drain(group):
        for dr, dc, copy in group:
            @pl.when(exists(dr, dc))
            def _():
                copy.wait_send()

    start(copies[:2])
    for copy in loads:
        copy.wait()

    lane = lane_of(rows)
    group = (lane % 64) // 16
    place = lane % 16
    right_part = lane < 64

    def pack(si, carry):
        total = jnp.zeros((rows, LANES), F32)
        for g in range(HALF):
            a = ext[si * ANG + HALF + g + 1, PAD : PAD + rows, 0:LANES].astype(F32)
            b = ext[si * ANG + HALF - g - 1, PAD : PAD + rows, cols - LANES : cols].astype(F32)
            total = jnp.where(right_part & (group == g), roll(a, 16 * g + 2), total)
            total = jnp.where((~right_part) & (group == g), roll(b, 16 * g + 78), total)
        sp[si + (si + 3) // 8] = total.astype(sp.dtype)
        return carry

    lax.fori_loop(0, ANG, pack, 0)
    sp[5] = jnp.where(right_part, ext[CENTER, PAD : PAD + rows, 0:LANES].astype(F32),
                      ext[CENTER, PAD : PAD + rows, cols - LANES : cols].astype(F32)).astype(sp.dtype)
    start(copies[2:])

    center = [ext[CENTER, PAD : PAD + rows, h * LANES : (h + 1) * LANES].astype(F32) for h in range(2)]
    ca, cb = center
    for ti in range(ANG):
        move = D0 * (ti - HALF)
        ra, rb = roll(ca, move), roll(cb, move)
        if move > 0:
            cen[ti, 0] = ra
            cen[ti, 1] = jnp.where(lane >= move, rb, ra)
        elif move < 0:
            cen[ti, 0] = jnp.where(lane < LANES + move, ra, rb)
            cen[ti, 1] = rb
        else:
            cen[ti, 0] = ca
            cen[ti, 1] = cb
    total = jnp.zeros((rows, LANES), F32)
    for g in range(HALF):
        m = D0 * (g + 1)
        total = jnp.where(right_part & (group == g), roll(cb, 16 * g - 126 + m), total)
        total = jnp.where((~right_part) & (group == g), roll(ca, 78 + 16 * g - m), total)
    cpack[...] = total
    pacc[...] = jnp.zeros_like(pacc)

    chunk = 16
    clane = lane_of(chunk)

    def terms(v0, side, down, s, tscale, middle):
        slope = tscale * side if s == 0 else (0.5 * s) * down + tscale * side
        error = v0 - middle
        weighted = slope * lax.rsqrt(1.0 + error * error)
        return weighted * slope, weighted * error

    def view_pass(signs):
        def body(ti, carry):
            tscale = 0.5 * (ti - HALF).astype(F32)
            for slot, s in enumerate(signs):
                low = 0 if s < 0 else PAD
                size = rows if s == 0 else rows + PAD
                for h in range(2):
                    fb[slot, h, low : low + size, :] = ext[
                        ANG * (s + HALF) + ti, low : low + size, h * LANES : (h + 1) * LANES].astype(F32)
            for at in range(0, rows, chunk):
                sums = [[None, None], [None, None]]
                middle = [cen[ti, h, at : at + chunk, :] for h in range(2)]
                for slot, s in enumerate(signs):
                    base = PAD + D0 * s + at
                    v0 = [fb[slot, h, base : base + chunk, :] for h in range(2)]
                    after = [roll(v, -1) for v in v0]
                    before = [roll(v, 1) for v in v0]
                    after[0] = jnp.where(clane == LANES - 1, after[1], after[0])
                    before[1] = jnp.where(clane == 0, before[0], before[1])
                    for h in range(2):
                        down = None
                        if s:
                            down = fb[slot, h, base + 1 : base + 1 + chunk, :] - fb[slot, h, base - 1 : base - 1 + chunk, :]
                        data, src = terms(v0[h], after[h] - before[h], down, s, tscale, middle[h])
                        sums[0][h] = data if sums[0][h] is None else sums[0][h] + data
                        sums[1][h] = src if sums[1][h] is None else sums[1][h] + src
                for f in range(2):
                    for h in range(2):
                        old = sums[f][h] if signs == (0,) else acc[ti, f, h, at : at + chunk, :] + sums[f][h]
                        acc[ti, f, h, at : at + chunk, :] = old
            return carry

        lax.fori_loop(0, ANG, body, 0)

    view_pass((0,))
    arrive(copies)
    for size in range(1, HALF + 1):
        view_pass((size, -size))

    flane = lane_of(full)
    fgroup, fplace, fright = (flane % 64) // 16, flane % 16, flane < 64
    ptscale = jnp.where(clane < 64, 0.5, -0.5) * ((clane % 64) // 16 + 1).astype(F32)
    for si in range(ANG):
        s = si - HALF
        slot = si + (si + 3) // 8
        low = 0 if s < 0 else PAD
        size = rows if s == 0 else rows + PAD
        part = slice(low, low + size)
        right, grp, plc = fright[part], fgroup[part], fplace[part]
        merged = jnp.where(right, col_r[slot, part, :].astype(F32), col_l[slot, part, :].astype(F32))
        for g in range(HALF):
            a = ext[si * ANG + HALF - g - 1, part, 0:LANES].astype(F32)
            b = ext[si * ANG + HALF + g + 1, part, cols - LANES : cols].astype(F32)
            merged = jnp.where(right & (grp == g) & (plc < 2), roll(b, 16 * g + 2), merged)
            merged = jnp.where((~right) & (grp == g) & (plc >= 14), roll(a, 16 * g + 78), merged)
        pb[part, :] = merged
        for at in range(0, rows, chunk):
            base = PAD + D0 * s + at
            v0 = pb[base : base + chunk, :]
            down = pb[base + 1 : base + 1 + chunk, :] - pb[base - 1 : base - 1 + chunk, :] if s else None
            data, src = terms(v0, roll(v0, -1) - roll(v0, 1), down, s, ptscale, cpack[at : at + chunk, :])
            pacc[0, at : at + chunk, :] += data
            pacc[1, at : at + chunk, :] += src

    for f in range(2):
        ta, tb = acc[HALF, f, 0], acc[HALF, f, 1]
        for ti in range(ANG):
            m = D0 * abs(ti - HALF)
            if m == 0:
                continue
            a, b = acc[ti, f, 0], acc[ti, f, 1]
            g = m // D0 - 1
            if ti > HALF:
                ra, rb = roll(a, -m), roll(b, -m)
                ta = ta + jnp.where(lane < LANES - m, ra, rb)
                tb = tb + jnp.where(lane <= LANES - 2 - m, rb, roll(pacc[f], 126 - m - 16 * g))
            else:
                ra, rb = roll(a, m), roll(b, m)
                ta = ta + jnp.where(lane >= m + 1, ra, roll(pacc[f], m - 78 - 16 * g))
                tb = tb + jnp.where(lane >= m, rb, ra)
        own[f, :, 0:LANES] = ta
        own[f, :, LANES : 2 * LANES] = tb

    coeff = damping + own[0] * (1.0 / VIEWS)
    source = own[1] * (-1.0 / VIEWS)

    frows, fcols = rows + 16, cols + 2 * LANES
    top = jnp.concatenate([col_l[5, 0:PAD, :], ext[CENTER, 0:PAD, :], col_r[5, 0:PAD, :]], axis=1).astype(F32)[8:16]
    mid = jnp.concatenate([col_l[5, PAD : PAD + rows, :], ext[CENTER, PAD : PAD + rows, :], col_r[5, PAD : PAD + rows, :]], axis=1).astype(F32)
    bot = jnp.concatenate([col_l[5, PAD + rows : full, :], ext[CENTER, PAD + rows : full, :], col_r[5, PAD + rows : full, :]], axis=1).astype(F32)[0:8]
    cf = jnp.concatenate([top, mid, bot], axis=0)
    gcol = lax.broadcasted_iota(jnp.int32, (frows, fcols), 1) + (c * cols - LANES)
    grow = lax.broadcasted_iota(jnp.int32, (frows, fcols), 0) + (r * rows - 8)

    def east(x):
        return pltpu.roll(x, fcols - 1, 1)

    def west(x):
        return pltpu.roll(x, 1, 1)

    def south(x):
        return pltpu.roll(x, frows - 1, 0)

    def north(x):
        return pltpu.roll(x, 1, 0)

    dx = east(cf) - cf
    dy = south(cf) - cf
    edge_e = jnp.where((gcol >= 0) & (gcol < ncol * cols - 1), jnp.exp(-dx * dx), 0.0)
    edge_s = jnp.where((grow >= 0) & (grow < nrow * rows - 1), jnp.exp(-dy * dy), 0.0)
    edge_w, edge_n = west(edge_e), north(edge_s)
    weights = smooth_weight * (edge_e + edge_w + edge_s + edge_n)

    inner = (slice(8, 8 + rows), slice(LANES, LANES + cols))
    zed = source / (coeff + weights[inner])
    zc[0] = zed
    zc[1] = coeff
    gpack[0] = jnp.where(right_part, zed[:, 0:LANES], roll(coeff[:, 0:LANES], 64))
    gpack[1] = jnp.where(right_part, roll(coeff[:, cols - LANES : cols], 64), zed[:, cols - LANES : cols])

    copies2 = []
    for index, (dr, dc) in enumerate(DIRS):
        if dc == 0:
            src = zc.at[:, pl.ds(0, 8), :] if dr < 0 else zc.at[:, pl.ds(rows - 8, 8), :]
            dst = ghost_d if dr < 0 else ghost_u
        elif dr == 0:
            src = gpack.at[0] if dc < 0 else gpack.at[1]
            dst = ghost_r if dc < 0 else ghost_l
        else:
            src = gpack.at[0 if dc < 0 else 1, pl.ds(0 if dr < 0 else rows - 8, 8), :]
            dst = corner.at[index - 4]
        copies2.append((dr, dc, pltpu.make_async_remote_copy(
            src_ref=src, dst_ref=dst, send_sem=send2.at[index], recv_sem=recv2.at[index],
            device_id=(r + dr, c + dc), device_id_type=pl.DeviceIdType.MESH)))
    start(copies2)
    drain(copies)
    arrive(copies2)

    zf = jnp.concatenate([
        jnp.concatenate([corner[3], ghost_u[0], corner[2]], axis=1),
        jnp.concatenate([ghost_l[...], zed, ghost_r[...]], axis=1),
        jnp.concatenate([corner[1], ghost_d[0], corner[0]], axis=1)], axis=0)
    one = jnp.ones((8, LANES), F32)
    kf = jnp.concatenate([
        jnp.concatenate([one, ghost_u[1], one], axis=1),
        jnp.concatenate([roll(ghost_l[...], 64), coeff, roll(ghost_r[...], 64)], axis=1),
        jnp.concatenate([one, ghost_d[1], one], axis=1)], axis=0)
    diag = kf + weights

    def operate(z):
        edges = edge_e * east(z) + edge_w * west(z) + edge_s * south(z) + edge_n * north(z)
        return diag * z - smooth_weight * edges

    wf = operate(zf)
    qf = wf / diag
    vf = operate(qf)
    w, q, v = wf[inner], qf[inner], vf[inner]
    rest = source - w
    y = zed - q
    wv = w - v
    sums = (zed * w, zed * rest, y * rest, q * rest, q * w, y * wv, y * v, q * v)
    line = lax.broadcasted_iota(jnp.int32, (1, LANES), 1)
    packed = jnp.zeros((1, LANES), F32)
    for i, x in enumerate(sums):
        x = jnp.sum(x, axis=0, keepdims=True)
        x = jnp.sum(x, axis=1, keepdims=True)
        packed = jnp.where(line == i, x, packed)
    redout[0] = packed
    redbuf[me] = packed

    def red_copy(i):
        peer = (me + i) % count
        return pltpu.make_async_remote_copy(
            src_ref=redout.at[0], dst_ref=redbuf.at[me], send_sem=rsend.at[0], recv_sem=rrecv.at[0],
            device_id=(peer // ncol, peer % ncol), device_id_type=pl.DeviceIdType.MESH)

    def cast_out(i, carry):
        red_copy(i).start()
        return carry

    lax.fori_loop(1, count, cast_out, 0)
    drain(copies2)
    others = redbuf.at[pl.ds(0, count - 1)]
    pltpu.make_async_copy(others, others, rrecv.at[0]).wait()
    pltpu.make_async_copy(others, others, rsend.at[0]).wait()
    totals = jnp.sum(redbuf[...], axis=0)
    b, e, f, g, h, k, l, m = [totals[:, i : i + 1] for i in range(8)]
    delta = e / b
    step0 = (e + b) / b
    rz0 = e + b
    rz1 = f - 2.0 * delta * g + delta * delta * h
    wu1 = k - 2.0 * delta * l + delta * delta * m
    beta = rz1 / rz0
    step1 = rz1 / (wu1 - beta * rz1 / step0)
    direction = (y - delta * q) + beta * zed
    image = (wv - delta * v) + beta * w
    inc[...] = step0 * zed + step1 * direction
    res[...] = (source - step0 * w) - step1 * image


def solution(mesh):
    nrow, ncol = mesh.shape["row"], mesh.shape["col"]

    def shards(views):
        _, rows, cols = views.shape
        full = PAD + rows + PAD
        bf = views.dtype
        return pl.pallas_call(
            functools.partial(kernel, nrow, ncol),
            out_shape=(jax.ShapeDtypeStruct((rows, cols), F32),) * 2,
            in_specs=[pl.BlockSpec(memory_space=pl.ANY)],
            out_specs=[pl.BlockSpec(memory_space=pltpu.VMEM)] * 2,
            scratch_shapes=[
                pltpu.VMEM((VIEWS, full, cols), bf),
                pltpu.VMEM((10, rows, LANES), bf),
                pltpu.VMEM((10, full, LANES), bf),
                pltpu.VMEM((10, full, LANES), bf),
                pltpu.VMEM((2, 2, full, LANES), F32),
                pltpu.VMEM((full, LANES), F32),
                pltpu.VMEM((ANG, 2, rows, LANES), F32),
                pltpu.VMEM((rows, LANES), F32),
                pltpu.VMEM((ANG, 2, 2, rows, LANES), F32),
                pltpu.VMEM((2, rows, LANES), F32),
                pltpu.VMEM((2, rows, cols), F32),
                pltpu.VMEM((2, rows, cols), F32),
                pltpu.VMEM((2, rows, LANES), F32),
                pltpu.VMEM((2, 8, cols), F32),
                pltpu.VMEM((2, 8, cols), F32),
                pltpu.VMEM((rows, LANES), F32),
                pltpu.VMEM((rows, LANES), F32),
                pltpu.VMEM((4, 8, LANES), F32),
                pltpu.VMEM((nrow * ncol, 1, LANES), F32),
                pltpu.VMEM((1, 1, LANES), F32),
                pltpu.SemaphoreType.DMA((ANG,)),
                pltpu.SemaphoreType.DMA((8,)),
                pltpu.SemaphoreType.DMA((8,)),
                pltpu.SemaphoreType.DMA((8,)),
                pltpu.SemaphoreType.DMA((8,)),
                pltpu.SemaphoreType.DMA((1,)),
                pltpu.SemaphoreType.DMA((1,)),
            ],
            compiler_params=pltpu.CompilerParams(collective_id=0, has_side_effects=True, vmem_limit_bytes=48 << 20),
        )(views)

    return jax.shard_map(
        shards,
        mesh=mesh,
        in_specs=(P(None, "row", "col"),),
        out_specs=(P("row", "col"), P("row", "col")),
        check_vma=False,
    )
```

time: 246 us -> 34.9 us (0.14)
  blocking collectives: 86.3 us -> 0 us
  other arithmetic: 77.3 us -> 0 us
  starting transfers between devices: 45.2 us -> 0 us
  Pallas kernels: 0 us -> 31.1 us
  local copies, waits for them, and re-layouts: 22.3 us -> 3 us
  waiting for transfers between devices: 7 us -> 0 us
  between operations: 7.04 us -> 0.65 us
    psum x2 -> x0, blocking collectives: 86.3 us -> none  [shards(): lax.psum((jnp.sum(residual * scaled_res), jnp.sum(image_res * scaled_res)...]
    div x3 -> x0, other arithmetic: 46.5 us -> none  [the longest x1 39.3 us: shards(): source = source_sum / VIEWS]
    ppermute x12 -> x0, starting transfers between devices: 45.2 us -> none  [the longest x6 37.1 us: with_halo(): before = lax.ppermute(last, axis, up)]
    pallas_call x0 -> x1, Pallas kernels: none -> 31.1 us  [shards(): pl.pallas_call(functools.partial(kernel, nrow, ncol), out_shape=(jax.Shap...]
    convert_element_type x28 -> x0, other arithmetic: 24.5 us -> none  [the longest x27 23.5 us: shards(): image = band[tindex].astype(jnp.float32)]
    slice x8 -> x0, local copies, waits for them, and re-layouts: 10.6 us -> none  [the longest x3 7.42 us: with_halo(): last = lax.slice_in_dim(array, length - width, length, axis=dim)]
    ppermute x4 -> x0, local copies, waits for them, and re-layouts: 8.2 us -> none  [the longest x2 4.11 us: with_halo(): before = lax.ppermute(last, axis, up)]
    ppermute x12 -> x0, waiting for transfers between devices: 7 us -> none  [the longest x6 6.99 us: with_halo(): before = lax.ppermute(last, axis, up)]
  transfers between devices with their start and end apart: 12 -> 0, of which waited for: 4 -> 0; matrix products, arithmetic and copies ran while one was open for 2% -> 0% of each run, Pallas kernels for 0% -> 0%
where the time goes in v1:
time: 34.9 us; the launch traced here: 34.7 us
  Pallas kernels  31.1 us (89%)
  local copies, waits for them, and re-layouts  3 us (9%)
  between operations  0.65 us (2%)
    pallas_call x1, Pallas kernels, shards(): pl.pallas_call(functools.partial(kernel, nrow, ncol), out_shape=(jax.Shap...  31.1 us
    unnamed x4, local copies, waits for them, and re-layouts  3 us

profile of v1, /device:TPU:0, one launch (start us, length us, event | category | flops | bytes accessed | tf_op | source)
XLA Modules:
  0.0 34.7 jit_solution(5277392165762928921)
XLA Ops:
  0.6 0.0 copy-start
  0.6 1.7 %copy-done = bf16[81,64,256]{2,1,0:T(8,128)(2,1)S(1)} copy-done((bf16[81,64,256]{2,1,0:T(8,128)(2,1)S(1)}, bf16[81,64,256]{2,1,0:T(8,128)(2,1)}, u32[]{:S(2)}) %copy-start) | copy-done | bytes 2654232
  2.4 31.1 %shard_map.30 = (f32[64,256]{1,0:T(8,128)S(1)}, f32[64,256]{1,0:T(8,128)S(1)}) custom-call(bf16[81,64,256]{2,1,0:T(8,128)(2,1)S(1)} %copy-done), custom_call_target="tpu_custom_call" | custom-call | tf_op jit(solution)/shard_map/pallas_call | solution.py:401
  33.4 0.6 %copy.5 = f32[64,256]{1,0:T(8,128)} copy(f32[64,256]{1,0:T(8,128)S(1)} %get-tuple-element.4) | data formatting | bytes 131072
  34.1 0.6 %copy.6 = f32[64,256]{1,0:T(8,128)} copy(f32[64,256]{1,0:T(8,128)S(1)} %get-tuple-element.5) | data formatting | bytes 131072
Async XLA Ops:
  0.6 1.8 %copy-start = (bf16[81,64,256]{2,1,0:T(8,128)(2,1)S(1)}, bf16[81,64,256]{2,1,0:T(8,128)(2,1)}, u32[]{:S(2)}) copy-start(bf16[81,64,256]{2,1,0:T(8,128)(2,1)} %views.1) | copy-start | bytes 7962628

commit v2 on v1

--- a/solution.py
+++ b/solution.py
@@ -72,15 +72,15 @@
     for ref, edge in ((col_r, c == ncol - 1), (col_l, c == 0)):
         @pl.when(edge)
         def _():
-            zero(ref, 0, 10, PAD, rows)
+            zero(ref, 0, 5, PAD, rows)
 
         @pl.when(edge | (r == 0))
         def _():
-            zero(ref, 0, 6, 0, PAD)
+            zero(ref, 0, 3, 0, PAD)
 
         @pl.when(edge | (r == nrow - 1))
         def _():
-            zero(ref, 5, 5, PAD + rows, PAD)
+            zero(ref, 2, 3, PAD + rows, PAD)
 
     for edge, ref in ((r == 0, ghost_u), (r == nrow - 1, ghost_d)):
         @pl.when(edge)
@@ -98,24 +98,33 @@
 
     pl.semaphore_wait(barrier, count - 1)
 
-    up_rows, down_rows = pl.ds(0, PAD), pl.ds(rows - PAD, PAD)
-    copies = []
-    for index, (dr, dc) in enumerate(DIRS):
-        if dc == 0:
+    row_copies = []
+    for size in range(HALF + 1):
+        reach = 8 if D0 * size + 1 <= 8 else PAD
+        for index, (dr, dc) in enumerate(DIRS[:2]):
+            if size == 0:
+                part = pl.ds(CENTER, 1)
+            else:
+                part = pl.ds(ANG * (HALF - dr * size), ANG)
             if dr < 0:
-                src, dst = views.at[pl.ds(40, 41), up_rows, :], ext.at[pl.ds(40, 41), pl.ds(PAD + rows, PAD), :]
+                src, dst = views.at[part, pl.ds(0, reach), :], ext.at[part, pl.ds(PAD + rows, reach), :]
             else:
-                src, dst = views.at[pl.ds(0, 41), down_rows, :], ext.at[pl.ds(0, 41), pl.ds(0, PAD), :]
+                src, dst = views.at[part, pl.ds(rows - reach, reach), :], ext.at[part, pl.ds(PAD - reach, reach), :]
+            row_copies.append((dr, dc, pltpu.make_async_remote_copy(
+                src_ref=src, dst_ref=dst, send_sem=send1.at[2 * size + index], recv_sem=recv1.at[2 * size + index],
+                device_id=(r + dr, c + dc), device_id_type=pl.DeviceIdType.MESH)))
+    col_copies = []
+    for index, (dr, dc) in enumerate(DIRS[2:]):
+        side = col_r if dc < 0 else col_l
+        mine = sp.at[0 if dc < 0 else 1]
+        if dr == 0:
+            src, dst = mine, side.at[:, pl.ds(PAD, rows), :]
+        elif dr < 0:
+            src, dst = mine.at[pl.ds(2, 3), pl.ds(0, PAD), :], side.at[pl.ds(2, 3), pl.ds(PAD + rows, PAD), :]
         else:
-            side = col_r if dc < 0 else col_l
-            if dr == 0:
-                src, dst = sp, side.at[:, pl.ds(PAD, rows), :]
-            elif dr < 0:
-                src, dst = sp.at[pl.ds(5, 5), up_rows, :], side.at[pl.ds(5, 5), pl.ds(PAD + rows, PAD), :]
-            else:
-                src, dst = sp.at[pl.ds(0, 6), down_rows, :], side.at[pl.ds(0, 6), pl.ds(0, PAD), :]
-        copies.append((dr, dc, pltpu.make_async_remote_copy(
-            src_ref=src, dst_ref=dst, send_sem=send1.at[index], recv_sem=recv1.at[index],
+            src, dst = mine.at[pl.ds(0, 3), pl.ds(rows - PAD, PAD), :], side.at[pl.ds(0, 3), pl.ds(0, PAD), :]
+        col_copies.append((dr, dc, pltpu.make_async_remote_copy(
+            src_ref=src, dst_ref=dst, send_sem=send1.at[10 + index], recv_sem=recv1.at[10 + index],
             device_id=(r + dr, c + dc), device_id_type=pl.DeviceIdType.MESH)))
 
     def start(group):
@@ -136,7 +145,7 @@
             def _():
                 copy.wait_send()
 
-    start(copies[:2])
+    start(row_copies)
     for copy in loads:
         copy.wait()
 
@@ -145,20 +154,27 @@
     place = lane % 16
     right_part = lane < 64
 
-    def pack(si, carry):
-        total = jnp.zeros((rows, LANES), F32)
-        for g in range(HALF):
-            a = ext[si * ANG + HALF + g + 1, PAD : PAD + rows, 0:LANES].astype(F32)
-            b = ext[si * ANG + HALF - g - 1, PAD : PAD + rows, cols - LANES : cols].astype(F32)
-            total = jnp.where(right_part & (group == g), roll(a, 16 * g + 2), total)
-            total = jnp.where((~right_part) & (group == g), roll(b, 16 * g + 78), total)
-        sp[si + (si + 3) // 8] = total.astype(sp.dtype)
-        return carry
-
-    lax.fori_loop(0, ANG, pack, 0)
-    sp[5] = jnp.where(right_part, ext[CENTER, PAD : PAD + rows, 0:LANES].astype(F32),
-                      ext[CENTER, PAD : PAD + rows, cols - LANES : cols].astype(F32)).astype(sp.dtype)
-    start(copies[2:])
+    for slot in range(5):
+        left = right = None
+        for half in range(2):
+            if slot == 2 and half == 1:
+                a = roll(ext[CENTER, PAD : PAD + rows, 0:LANES].astype(F32), 64)
+                b = ext[CENTER, PAD : PAD + rows, cols - LANES : cols].astype(F32)
+            else:
+                si = (0, 2, 4, 5, 7)[slot] + half
+                a = b = None
+                for g in range(HALF):
+                    x = ext[si * ANG + HALF + g + 1, PAD : PAD + rows, 0:LANES].astype(F32)
+                    x = roll(x, 16 * g + 2 + 64 * half)
+                    a = x if a is None else jnp.where(group == g, x, a)
+                    x = ext[si * ANG + HALF - g - 1, PAD : PAD + rows, cols - LANES : cols].astype(F32)
+                    x = roll(x, 16 * g + 14 + 64 * half)
+                    b = x if b is None else jnp.where(group == g, x, b)
+            left = a if half == 0 else jnp.where(right_part, left, a)
+            right = b if half == 0 else jnp.where(right_part, right, b)
+        sp[0, slot] = left.astype(sp.dtype)
+        sp[1, slot] = right.astype(sp.dtype)
+    start(col_copies)
 
     center = [ext[CENTER, PAD : PAD + rows, h * LANES : (h + 1) * LANES].astype(F32) for h in range(2)]
     ca, cb = center
@@ -226,21 +242,23 @@
         lax.fori_loop(0, ANG, body, 0)
 
     view_pass((0,))
-    arrive(copies)
     for size in range(1, HALF + 1):
+        arrive(row_copies[2 * size : 2 * size + 2])
         view_pass((size, -size))
+    arrive(row_copies[:2] + col_copies)
 
     flane = lane_of(full)
     fgroup, fplace, fright = (flane % 64) // 16, flane % 16, flane < 64
     ptscale = jnp.where(clane < 64, 0.5, -0.5) * ((clane % 64) // 16 + 1).astype(F32)
     for si in range(ANG):
         s = si - HALF
-        slot = si + (si + 3) // 8
+        slot, half = ((0, 0), (0, 1), (1, 0), (1, 1), (2, 0), (3, 0), (3, 1), (4, 0), (4, 1))[si]
         low = 0 if s < 0 else PAD
         size = rows if s == 0 else rows + PAD
         part = slice(low, low + size)
         right, grp, plc = fright[part], fgroup[part], fplace[part]
-        merged = jnp.where(right, col_r[slot, part, :].astype(F32), col_l[slot, part, :].astype(F32))
+        x, z = col_r[slot, part, :].astype(F32), col_l[slot, part, :].astype(F32)
+        merged = jnp.where(right, roll(x, 64) if half else x, z if half else roll(z, 64))
         for g in range(HALF):
             a = ext[si * ANG + HALF - g - 1, part, 0:LANES].astype(F32)
             b = ext[si * ANG + HALF + g + 1, part, cols - LANES : cols].astype(F32)
@@ -278,10 +296,11 @@
     source = own[1] * (-1.0 / VIEWS)
 
     frows, fcols = rows + 16, cols + 2 * LANES
-    top = jnp.concatenate([col_l[5, 0:PAD, :], ext[CENTER, 0:PAD, :], col_r[5, 0:PAD, :]], axis=1).astype(F32)[8:16]
-    mid = jnp.concatenate([col_l[5, PAD : PAD + rows, :], ext[CENTER, PAD : PAD + rows, :], col_r[5, PAD : PAD + rows, :]], axis=1).astype(F32)
-    bot = jnp.concatenate([col_l[5, PAD + rows : full, :], ext[CENTER, PAD + rows : full, :], col_r[5, PAD + rows : full, :]], axis=1).astype(F32)[0:8]
-    cf = jnp.concatenate([top, mid, bot], axis=0)
+    bands = []
+    for part in (slice(0, PAD), slice(PAD, PAD + rows), slice(PAD + rows, full)):
+        bands.append(jnp.concatenate([
+            col_l[2, part, :].astype(F32), ext[CENTER, part, :].astype(F32), roll(col_r[2, part, :].astype(F32), 64)], axis=1))
+    cf = jnp.concatenate([bands[0][8:16], bands[1], bands[2][0:8]], axis=0)
     gcol = lax.broadcasted_iota(jnp.int32, (frows, fcols), 1) + (c * cols - LANES)
     grow = lax.broadcasted_iota(jnp.int32, (frows, fcols), 0) + (r * rows - 8)
 
@@ -326,7 +345,7 @@
             src_ref=src, dst_ref=dst, send_sem=send2.at[index], recv_sem=recv2.at[index],
             device_id=(r + dr, c + dc), device_id_type=pl.DeviceIdType.MESH)))
     start(copies2)
-    drain(copies)
+    drain(row_copies + col_copies)
     arrive(copies2)
 
     zf = jnp.concatenate([
@@ -401,13 +420,13 @@
         return pl.pallas_call(
             functools.partial(kernel, nrow, ncol),
             out_shape=(jax.ShapeDtypeStruct((rows, cols), F32),) * 2,
-            in_specs=[pl.BlockSpec(memory_space=pl.ANY)],
+            in_specs=[pl.BlockSpec(memory_space=pltpu.HBM)],
             out_specs=[pl.BlockSpec(memory_space=pltpu.VMEM)] * 2,
             scratch_shapes=[
                 pltpu.VMEM((VIEWS, full, cols), bf),
-                pltpu.VMEM((10, rows, LANES), bf),
-                pltpu.VMEM((10, full, LANES), bf),
-                pltpu.VMEM((10, full, LANES), bf),
+                pltpu.VMEM((2, 5, rows, LANES), bf),
+                pltpu.VMEM((5, full, LANES), bf),
+                pltpu.VMEM((5, full, LANES), bf),
                 pltpu.VMEM((2, 2, full, LANES), F32),
                 pltpu.VMEM((full, LANES), F32),
                 pltpu.VMEM((ANG, 2, rows, LANES), F32),
@@ -425,8 +444,8 @@
                 pltpu.VMEM((nrow * ncol, 1, LANES), F32),
                 pltpu.VMEM((1, 1, LANES), F32),
                 pltpu.SemaphoreType.DMA((ANG,)),
-                pltpu.SemaphoreType.DMA((8,)),
-                pltpu.SemaphoreType.DMA((8,)),
+                pltpu.SemaphoreType.DMA((16,)),
+                pltpu.SemaphoreType.DMA((16,)),
                 pltpu.SemaphoreType.DMA((8,)),
                 pltpu.SemaphoreType.DMA((8,)),
                 pltpu.SemaphoreType.DMA((1,)),

time: 34.9 us -> 30.3 us (0.87)
  Pallas kernels: 31.1 us -> 26.5 us
    pallas_call x1, Pallas kernels: 31.1 us -> 26.5 us  [shards(): pl.pallas_call(functools.partial(kernel, nrow, ncol), out_shape=(jax.Shap...]
where the time goes in v2:
time: 30.3 us; the launch traced here: 30.1 us
  Pallas kernels  26.5 us (87%)
  local copies, waits for them, and re-layouts  3 us (10%)
  between operations  0.65 us (2%)
    pallas_call x1, Pallas kernels, shards(): pl.pallas_call(functools.partial(kernel, nrow, ncol), out_shape=(jax.Shap...  26.5 us
    unnamed x4, local copies, waits for them, and re-layouts  3 us

profile of v2, /device:TPU:0, one launch (start us, length us, event | category | flops | bytes accessed | tf_op | source)
XLA Modules:
  0.0 30.1 jit_solution(1703086736944046292)
XLA Ops:
  0.6 0.0 copy-start
  0.6 1.7 %copy-done = bf16[81,64,256]{2,1,0:T(8,128)(2,1)S(1)} copy-done((bf16[81,64,256]{2,1,0:T(8,128)(2,1)S(1)}, bf16[81,64,256]{2,1,0:T(8,128)(2,1)}, u32[]{:S(2)}) %copy-start) | copy-done | bytes 2654232
  2.4 26.5 %shard_map.30 = (f32[64,256]{1,0:T(8,128)S(1)}, f32[64,256]{1,0:T(8,128)S(1)}) custom-call(bf16[81,64,256]{2,1,0:T(8,128)(2,1)S(1)} %copy-done), custom_call_target="tpu_custom_call" | custom-call | tf_op jit(solution)/shard_map/pallas_call | solution.py:420
  28.9 0.6 %copy.5 = f32[64,256]{1,0:T(8,128)} copy(f32[64,256]{1,0:T(8,128)S(1)} %get-tuple-element.4) | data formatting | bytes 131072
  29.5 0.6 %copy.6 = f32[64,256]{1,0:T(8,128)} copy(f32[64,256]{1,0:T(8,128)S(1)} %get-tuple-element.5) | data formatting | bytes 131072
Async XLA Ops:
  0.6 1.8 %copy-start = (bf16[81,64,256]{2,1,0:T(8,128)(2,1)S(1)}, bf16[81,64,256]{2,1,0:T(8,128)(2,1)}, u32[]{:S(2)}) copy-start(bf16[81,64,256]{2,1,0:T(8,128)(2,1)} %views.1) | copy-start | bytes 7962628

commit v3 on v2

--- a/solution.py
+++ b/solution.py
@@ -28,7 +28,7 @@
     return lax.broadcasted_iota(jnp.int32, (rows, LANES), 1)
 
 
-def kernel(nrow, ncol, views, inc, res, ext, sp, col_r, col_l, fb, pb, cen, cpack, acc, pacc, own, zc, gpack,
+def kernel(nrow, ncol, views, out, ext, sp, col_r, col_l, fb, pb, cen, cpack, acc, pacc, own, zc, gpack,
            ghost_u, ghost_d, ghost_l, ghost_r, corner, redbuf, redout, load_sem, send1, recv1, send2, recv2, rsend, rrecv):
     rows, cols = views.shape[1], views.shape[2]
     r, c = lax.axis_index("row"), lax.axis_index("col")
@@ -96,7 +96,6 @@
         def _():
             corner[index] = jnp.zeros((8, LANES), F32)
 
-    pl.semaphore_wait(barrier, count - 1)
 
     row_copies = []
     for size in range(HALF + 1):
@@ -145,7 +144,6 @@
             def _():
                 copy.wait_send()
 
-    start(row_copies)
     for copy in loads:
         copy.wait()
 
@@ -174,6 +172,8 @@
             right = b if half == 0 else jnp.where(right_part, right, b)
         sp[0, slot] = left.astype(sp.dtype)
         sp[1, slot] = right.astype(sp.dtype)
+    pl.semaphore_wait(barrier, count - 1)
+    start(row_copies)
     start(col_copies)
 
     center = [ext[CENTER, PAD : PAD + rows, h * LANES : (h + 1) * LANES].astype(F32) for h in range(2)]
@@ -207,32 +207,36 @@
         weighted = slope * lax.rsqrt(1.0 + error * error)
         return weighted * slope, weighted * error
 
+    def view_step(ti, tscale, slot, s, at, middle, sums):
+        base = PAD + D0 * s + at
+        v0 = [fb[slot, h, base : base + chunk, :] for h in range(2)]
+        after = [roll(v, -1) for v in v0]
+        before = [roll(v, 1) for v in v0]
+        after[0] = jnp.where(clane == LANES - 1, after[1], after[0])
+        before[1] = jnp.where(clane == 0, before[0], before[1])
+        for h in range(2):
+            down = None
+            if s:
+                down = fb[slot, h, base + 1 : base + 1 + chunk, :] - fb[slot, h, base - 1 : base - 1 + chunk, :]
+            data, src = terms(v0[h], after[h] - before[h], down, s, tscale, middle[h])
+            sums[0][h] = data if sums[0][h] is None else sums[0][h] + data
+            sums[1][h] = src if sums[1][h] is None else sums[1][h] + src
+
+    def widen(ti, slot, s, low, high):
+        for h in range(2):
+            fb[slot, h, low:high, :] = ext[ANG * (s + HALF) + ti, low:high, h * LANES : (h + 1) * LANES].astype(F32)
+
     def view_pass(signs):
         def body(ti, carry):
             tscale = 0.5 * (ti - HALF).astype(F32)
             for slot, s in enumerate(signs):
-                low = 0 if s < 0 else PAD
-                size = rows if s == 0 else rows + PAD
-                for h in range(2):
-                    fb[slot, h, low : low + size, :] = ext[
-                        ANG * (s + HALF) + ti, low : low + size, h * LANES : (h + 1) * LANES].astype(F32)
+                widen(ti, slot, s, PAD, PAD + rows)
             for at in range(0, rows, chunk):
                 sums = [[None, None], [None, None]]
                 middle = [cen[ti, h, at : at + chunk, :] for h in range(2)]
                 for slot, s in enumerate(signs):
-                    base = PAD + D0 * s + at
-                    v0 = [fb[slot, h, base : base + chunk, :] for h in range(2)]
-                    after = [roll(v, -1) for v in v0]
-                    before = [roll(v, 1) for v in v0]
-                    after[0] = jnp.where(clane == LANES - 1, after[1], after[0])
-                    before[1] = jnp.where(clane == 0, before[0], before[1])
-                    for h in range(2):
-                        down = None
-                        if s:
-                            down = fb[slot, h, base + 1 : base + 1 + chunk, :] - fb[slot, h, base - 1 : base - 1 + chunk, :]
-                        data, src = terms(v0[h], after[h] - before[h], down, s, tscale, middle[h])
-                        sums[0][h] = data if sums[0][h] is None else sums[0][h] + data
-                        sums[1][h] = src if sums[1][h] is None else sums[1][h] + src
+                    if not ((s > 0 and at == rows - chunk) or (s < 0 and at == 0)):
+                        view_step(ti, tscale, slot, s, at, middle, sums)
                 for f in range(2):
                     for h in range(2):
                         old = sums[f][h] if signs == (0,) else acc[ti, f, h, at : at + chunk, :] + sums[f][h]
@@ -243,9 +247,26 @@
 
     view_pass((0,))
     for size in range(1, HALF + 1):
-        arrive(row_copies[2 * size : 2 * size + 2])
         view_pass((size, -size))
-    arrive(row_copies[:2] + col_copies)
+    arrive(row_copies)
+
+    def edge_pass(ti, carry):
+        tscale = 0.5 * (ti - HALF).astype(F32)
+        for sign, at in ((1, rows - chunk), (-1, 0)):
+            sums = [[acc[ti, f, h, at : at + chunk, :] for h in range(2)] for f in range(2)]
+            middle = [cen[ti, h, at : at + chunk, :] for h in range(2)]
+            for size in range(1, HALF + 1):
+                slot = 2 * (size - 1) + (sign < 0)
+                low = PAD + at if sign > 0 else 0
+                widen(ti, slot, sign * size, low, low + 2 * PAD)
+                view_step(ti, tscale, slot, sign * size, at, middle, sums)
+            for f in range(2):
+                for h in range(2):
+                    acc[ti, f, h, at : at + chunk, :] = sums[f][h]
+        return carry
+
+    lax.fori_loop(0, ANG, edge_pass, 0)
+    arrive(col_copies)
 
     flane = lane_of(full)
     fgroup, fplace, fright = (flane % 64) // 16, flane % 16, flane < 64
@@ -406,8 +427,8 @@
     step1 = rz1 / (wu1 - beta * rz1 / step0)
     direction = (y - delta * q) + beta * zed
     image = (wv - delta * v) + beta * w
-    inc[...] = step0 * zed + step1 * direction
-    res[...] = (source - step0 * w) - step1 * image
+    out[0] = step0 * zed + step1 * direction
+    out[1] = (source - step0 * w) - step1 * image
 
 
 def solution(mesh):
@@ -417,17 +438,17 @@
         _, rows, cols = views.shape
         full = PAD + rows + PAD
         bf = views.dtype
-        return pl.pallas_call(
+        out = pl.pallas_call(
             functools.partial(kernel, nrow, ncol),
-            out_shape=(jax.ShapeDtypeStruct((rows, cols), F32),) * 2,
+            out_shape=jax.ShapeDtypeStruct((2, rows, cols), F32),
             in_specs=[pl.BlockSpec(memory_space=pltpu.HBM)],
-            out_specs=[pl.BlockSpec(memory_space=pltpu.VMEM)] * 2,
+            out_specs=pl.BlockSpec(memory_space=pltpu.VMEM),
             scratch_shapes=[
                 pltpu.VMEM((VIEWS, full, cols), bf),
                 pltpu.VMEM((2, 5, rows, LANES), bf),
                 pltpu.VMEM((5, full, LANES), bf),
                 pltpu.VMEM((5, full, LANES), bf),
-                pltpu.VMEM((2, 2, full, LANES), F32),
+                pltpu.VMEM((8, 2, full, LANES), F32),
                 pltpu.VMEM((full, LANES), F32),
                 pltpu.VMEM((ANG, 2, rows, LANES), F32),
                 pltpu.VMEM((rows, LANES), F32),
@@ -452,7 +473,8 @@
                 pltpu.SemaphoreType.DMA((1,)),
             ],
             compiler_params=pltpu.CompilerParams(collective_id=0, has_side_effects=True, vmem_limit_bytes=48 << 20),
-        )(views)
+        )(pltpu.with_memory_space_constraint(views, pltpu.HBM))
+        return out[0], out[1]
 
     return jax.shard_map(
         shards,

time: 30.3 us -> 26.9 us (0.89)
  local copies, waits for them, and re-layouts: 3 us -> 0.66 us
  Pallas kernels: 26.5 us -> 25.5 us
    unnamed x4 -> x0, local copies, waits for them, and re-layouts: 3 us -> none
    pallas_call x1, Pallas kernels: 26.5 us -> 25.5 us  [shards(): pl.pallas_call(functools.partial(kernel, nrow, ncol), out_shape=jax.Shape...]
    squeeze x0 -> x1, local copies, waits for them, and re-layouts: none -> 0.66 us  [shards(): return (out[0], out[1])]
where the time goes in v3:
time: 26.9 us; the launch traced here: 26.8 us
  Pallas kernels  25.5 us (95%)
  local copies, waits for them, and re-layouts  0.66 us (2%)
  between operations  0.64 us (2%)
    pallas_call x1, Pallas kernels, shards(): pl.pallas_call(functools.partial(kernel, nrow, ncol), out_shape=jax.Shape...  25.5 us
    squeeze x1, local copies, waits for them, and re-layouts, shards(): return (out[0], out[1])  0.66 us

profile of v3, /device:TPU:0, one launch (start us, length us, event | category | flops | bytes accessed | tf_op | source)
XLA Modules:
  0.0 26.8 jit_solution(11406329734916725586)
XLA Ops:
  0.6 25.5 %shard_map.30 = f32[2,64,256]{2,1,0:T(8,128)S(1)} custom-call(bf16[81,64,256]{2,1,0:T(8,128)(2,1)} %views.1), custom_call_target="tpu_custom_call" | custom-call | tf_op jit(solution)/shard_map/pallas_call | solution.py:441
  26.1 0.7 %slice_bitcast_fusion = (f32[64,256]{1,0:T(8,128)}, f32[64,256]{1,0:T(8,128)}) fusion(f32[2,64,256]{2,1,0:T(8,128)S(1)} %shard_map.30), kind=kLoop, calls=%fused_computation | loop fusion | bytes 262144 | tf_op jit(solution)/shard_map/squeeze | solution.py:477

commit v4 on v3

--- a/solution.py
+++ b/solution.py
@@ -144,6 +144,8 @@
             def _():
                 copy.wait_send()
 
+    pl.semaphore_wait(barrier, count - 1)
+    start(row_copies)
     for copy in loads:
         copy.wait()
 
@@ -172,8 +174,6 @@
             right = b if half == 0 else jnp.where(right_part, right, b)
         sp[0, slot] = left.astype(sp.dtype)
         sp[1, slot] = right.astype(sp.dtype)
-    pl.semaphore_wait(barrier, count - 1)
-    start(row_copies)
     start(col_copies)
 
     center = [ext[CENTER, PAD : PAD + rows, h * LANES : (h + 1) * LANES].astype(F32) for h in range(2)]
@@ -248,7 +248,70 @@
     view_pass((0,))
     for size in range(1, HALF + 1):
         view_pass((size, -size))
-    arrive(row_copies)
+    arrive(row_copies[:2] + col_copies)
+    frows, fcols = rows + 16, cols + 2 * LANES
+    bands = []
+    for part in (slice(0, PAD), slice(PAD, PAD + rows), slice(PAD + rows, full)):
+        bands.append(jnp.concatenate([
+            col_l[2, part, :].astype(F32), ext[CENTER, part, :].astype(F32), roll(col_r[2, part, :].astype(F32), 64)], axis=1))
+    cf = jnp.concatenate([bands[0][8:16], bands[1], bands[2][0:8]], axis=0)
+    gcol = lax.broadcasted_iota(jnp.int32, (frows, fcols), 1) + (c * cols - LANES)
+    grow = lax.broadcasted_iota(jnp.int32, (frows, fcols), 0) + (r * rows - 8)
+
+    def east(x):
+        return pltpu.roll(x, fcols - 1, 1)
+
+    def west(x):
+        return pltpu.roll(x, 1, 1)
+
+    def south(x):
+        return pltpu.roll(x, frows - 1, 0)
+
+    def north(x):
+        return pltpu.roll(x, 1, 0)
+
+    dx = east(cf) - cf
+    dy = south(cf) - cf
+    edge_e = jnp.where((gcol >= 0) & (gcol < ncol * cols - 1), jnp.exp(-dx * dx), 0.0)
+    edge_s = jnp.where((grow >= 0) & (grow < nrow * rows - 1), jnp.exp(-dy * dy), 0.0)
+    edge_w, edge_n = west(edge_e), north(edge_s)
+    weights = smooth_weight * (edge_e + edge_w + edge_s + edge_n)
+
+    flane = lane_of(full)
+    fgroup, fplace, fright = (flane % 64) // 16, flane % 16, flane < 64
+    ptscale = jnp.where(clane < 64, 0.5, -0.5) * ((clane % 64) // 16 + 1).astype(F32)
+
+    def packed_rows(si, low, high):
+        slot, half = ((0, 0), (0, 1), (1, 0), (1, 1), (2, 0), (3, 0), (3, 1), (4, 0), (4, 1))[si]
+        part = slice(low, high)
+        right, grp, plc = fright[part], fgroup[part], fplace[part]
+        x, z = col_r[slot, part, :].astype(F32), col_l[slot, part, :].astype(F32)
+        merged = jnp.where(right, roll(x, 64) if half else x, z if half else roll(z, 64))
+        for g in range(HALF):
+            a = ext[si * ANG + HALF - g - 1, part, 0:LANES].astype(F32)
+            b = ext[si * ANG + HALF + g + 1, part, cols - LANES : cols].astype(F32)
+            merged = jnp.where(right & (grp == g) & (plc < 2), roll(b, 16 * g + 2), merged)
+            merged = jnp.where((~right) & (grp == g) & (plc >= 14), roll(a, 16 * g + 78), merged)
+        pb[si, part, :] = merged
+
+    def packed_step(si, at):
+        s = si - HALF
+        base = PAD + D0 * s + at
+        v0 = pb[si, base : base + chunk, :]
+        down = pb[si, base + 1 : base + 1 + chunk, :] - pb[si, base - 1 : base - 1 + chunk, :] if s else None
+        data, src = terms(v0, roll(v0, -1) - roll(v0, 1), down, s, ptscale, cpack[at : at + chunk, :])
+        pacc[0, at : at + chunk, :] += data
+        pacc[1, at : at + chunk, :] += src
+
+    def last_rows(si):
+        return None if si == HALF else rows - chunk if si > HALF else 0
+
+    for si in range(ANG):
+        packed_rows(si, PAD, PAD + rows)
+        for at in range(0, rows, chunk):
+            if at != last_rows(si):
+                packed_step(si, at)
+    arrive(row_copies[2:])
 
     def edge_pass(ti, carry):
         tscale = 0.5 * (ti - HALF).astype(F32)
@@ -266,33 +329,11 @@
         return carry
 
     lax.fori_loop(0, ANG, edge_pass, 0)
-    arrive(col_copies)
-
-    flane = lane_of(full)
-    fgroup, fplace, fright = (flane % 64) // 16, flane % 16, flane < 64
-    ptscale = jnp.where(clane < 64, 0.5, -0.5) * ((clane % 64) // 16 + 1).astype(F32)
     for si in range(ANG):
-        s = si - HALF
-        slot, half = ((0, 0), (0, 1), (1, 0), (1, 1), (2, 0), (3, 0), (3, 1), (4, 0), (4, 1))[si]
-        low = 0 if s < 0 else PAD
-        size = rows if s == 0 else rows + PAD
-        part = slice(low, low + size)
-        right, grp, plc = fright[part], fgroup[part], fplace[part]
-        x, z = col_r[slot, part, :].astype(F32), col_l[slot, part, :].astype(F32)
-        merged = jnp.where(right, roll(x, 64) if half else x, z if half else roll(z, 64))
-        for g in range(HALF):
-            a = ext[si * ANG + HALF - g - 1, part, 0:LANES].astype(F32)
-            b = ext[si * ANG + HALF + g + 1, part, cols - LANES : cols].astype(F32)
-            merged = jnp.where(right & (grp == g) & (plc < 2), roll(b, 16 * g + 2), merged)
-            merged = jnp.where((~right) & (grp == g) & (plc >= 14), roll(a, 16 * g + 78), merged)
-        pb[part, :] = merged
-        for at in range(0, rows, chunk):
-            base = PAD + D0 * s + at
-            v0 = pb[base : base + chunk, :]
-            down = pb[base + 1 : base + 1 + chunk, :] - pb[base - 1 : base - 1 + chunk, :] if s else None
-            data, src = terms(v0, roll(v0, -1) - roll(v0, 1), down, s, ptscale, cpack[at : at + chunk, :])
-            pacc[0, at : at + chunk, :] += data
-            pacc[1, at : at + chunk, :] += src
+        if si != HALF:
+            low = PAD + rows if si > HALF else 0
+            packed_rows(si, low, low + PAD)
+            packed_step(si, last_rows(si))
 
     for f in range(2):
         ta, tb = acc[HALF, f, 0], acc[HALF, f, 1]
@@ -316,34 +357,6 @@
     coeff = damping + own[0] * (1.0 / VIEWS)
     source = own[1] * (-1.0 / VIEWS)
 
-    frows, fcols = rows + 16, cols + 2 * LANES
-    bands = []
-    for part in (slice(0, PAD), slice(PAD, PAD + rows), slice(PAD + rows, full)):
-        bands.append(jnp.concatenate([
-            col_l[2, part, :].astype(F32), ext[CENTER, part, :].astype(F32), roll(col_r[2, part, :].astype(F32), 64)], axis=1))
-    cf = jnp.concatenate([bands[0][8:16], bands[1], bands[2][0:8]], axis=0)
-    gcol = lax.broadcasted_iota(jnp.int32, (frows, fcols), 1) + (c * cols - LANES)
-    grow = lax.broadcasted_iota(jnp.int32, (frows, fcols), 0) + (r * rows - 8)
-
-    def east(x):
-        return pltpu.roll(x, fcols - 1, 1)
-
-    def west(x):
-        return pltpu.roll(x, 1, 1)
-
-    def south(x):
-        return pltpu.roll(x, frows - 1, 0)
-
-    def north(x):
-        return pltpu.roll(x, 1, 0)
-
-    dx = east(cf) - cf
-    dy = south(cf) - cf
-    edge_e = jnp.where((gcol >= 0) & (gcol < ncol * cols - 1), jnp.exp(-dx * dx), 0.0)
-    edge_s = jnp.where((grow >= 0) & (grow < nrow * rows - 1), jnp.exp(-dy * dy), 0.0)
-    edge_w, edge_n = west(edge_e), north(edge_s)
-    weights = smooth_weight * (edge_e + edge_w + edge_s + edge_n)
-
     inner = (slice(8, 8 + rows), slice(LANES, LANES + cols))
     zed = source / (coeff + weights[inner])
     zc[0] = zed
@@ -449,7 +462,7 @@
                 pltpu.VMEM((5, full, LANES), bf),
                 pltpu.VMEM((5, full, LANES), bf),
                 pltpu.VMEM((8, 2, full, LANES), F32),
-                pltpu.VMEM((full, LANES), F32),
+                pltpu.VMEM((ANG, full, LANES), F32),
                 pltpu.VMEM((ANG, 2, rows, LANES), F32),
                 pltpu.VMEM((rows, LANES), F32),
                 pltpu.VMEM((ANG, 2, 2, rows, LANES), F32),

time: 26.9 us -> 25.7 us (0.955)
  Pallas kernels: 25.5 us -> 24.3 us
    pallas_call x1, Pallas kernels: 25.5 us -> 24.3 us  [shards(): pl.pallas_call(functools.partial(kernel, nrow, ncol), out_shape=jax.Shape...]
where the time goes in v4:
time: 25.7 us; the launch traced here: 25.6 us
  Pallas kernels  24.3 us (95%)
  local copies, waits for them, and re-layouts  0.66 us (3%)
  between operations  0.64 us (2%)
    pallas_call x1, Pallas kernels, shards(): pl.pallas_call(functools.partial(kernel, nrow, ncol), out_shape=jax.Shape...  24.3 us
    squeeze x1, local copies, waits for them, and re-layouts, shards(): return (out[0], out[1])  0.66 us

profile of v4, /device:TPU:0, one launch (start us, length us, event | category | flops | bytes accessed | tf_op | source)
XLA Modules:
  0.0 25.6 jit_solution(4863136821584446027)
XLA Ops:
  0.6 24.3 %shard_map.30 = f32[2,64,256]{2,1,0:T(8,128)S(1)} custom-call(bf16[81,64,256]{2,1,0:T(8,128)(2,1)} %views.1), custom_call_target="tpu_custom_call" | custom-call | tf_op jit(solution)/shard_map/pallas_call | solution.py:454
  24.9 0.7 %slice_bitcast_fusion = (f32[64,256]{1,0:T(8,128)}, f32[64,256]{1,0:T(8,128)}) fusion(f32[2,64,256]{2,1,0:T(8,128)S(1)} %shard_map.30), kind=kLoop, calls=%fused_computation | loop fusion | bytes 262144 | tf_op jit(solution)/shard_map/squeeze | solution.py:490
